TPU v7x, 256 devices: a whole 4x4x8 slice. The times are simulated.
256 devices in a mesh: tmpl: 2 (over core), row: 128 (over x, y, z).
Axes of the slice: x: 4, y: 4, z: 8, core: 2. Of those that a mesh axis runs over, the one named last changes fastest.
Arguments:
- pair_maps: bfloat16 [2, 2048, 2048, 64], P('tmpl', 'row'), may hold values from -6 to 6
- crop_tiles: int32 [2, 8], P('tmpl'), may hold values from 0 to 15, as said below
- full_length: int32 [1], replicated, may hold values from 1536 to 2048
- proj_weight: bfloat16 [2, 64, 320], replicated, may hold values from -0.75 to 0.75
- out_weight: bfloat16 [2, 64, 64], replicated, may hold values from -0.75 to 0.75
- final_weight: bfloat16 [64, 128], replicated, may hold values from -0.75 to 0.75
Outputs:
- embedding: bfloat16 [128, 1024, 1024], P(None, 'row')
Inputs may be any that keep to these rules, and one draw needn't show every extreme that they name: Each row of crop_tiles names 8 different tiles of the 16, in increasing order; its last 4 entries are the tiles 16 - 8 // 2 to 15.
All inputs are finite; a program needn't handle non-finite values.
Results may differ from a plain program's by a relative error of at most 0.014.
Values may be sent and summed in bfloat16 or wider, within the bound.
No kernel may reach another device: no remote copies, remote signals or barrier semaphores. Data moves between devices by JAX's collectives and lax.ppermute only.
A program may use at most 64 MiB of HBM per device.

v0:
```python
import jax
import jax.numpy as jnp
from jax import lax
from jax.sharding import PartitionSpec as P

CH = 64
CROP = 1024
TILE = 128
NLAYER = 2
FULL = 2048
EPSILON = 1e-05


def from_partner(value, axis, bit):
    mask = 2**bit
    pairs = [(source, source ^ mask) for source in range(lax.axis_size(axis))]
    return lax.ppermute(value, axis, pairs)


def channel_norm(values):
    center = values - jnp.mean(values, axis=0, keepdims=True)
    spread = jnp.mean(center * center, axis=0, keepdims=True)
    return center * lax.rsqrt(spread + EPSILON)


def on_device(pair_maps, crop_tiles, full_length, proj_weight, out_weight, final_weight):
    row_count = lax.axis_size("row")
    my_index = lax.axis_index("row")
    pair_local = pair_maps[0]
    crop_ids = crop_tiles[0]
    local_rows = pair_local.shape[0]
    col_width = CROP // row_count
    parts_count = max(1, row_count // CH)
    per_group = CH * parts_count // row_count
    groups = CH // per_group
    part_rows = CROP // parts_count
    steps_crop = jnp.arange(CROP, dtype=jnp.int32)
    position = crop_ids[steps_crop // TILE] * TILE + steps_crop % TILE
    usable = (position < full_length[0]).astype(jnp.float32)
    col_usable = lax.dynamic_slice_in_dim(usable, my_index * col_width, col_width)
    pair_mask = col_usable[:, None] * usable[None, :]
    columns = pair_local.reshape(local_rows, FULL // TILE, TILE, CH)[:, crop_ids]
    columns = columns.reshape(local_rows, CROP * CH)
    received = lax.all_to_all(columns, "row", split_axis=1, concat_axis=0, tiled=True)
    cropped = received.reshape(FULL // TILE, TILE, col_width * CH)[crop_ids]
    current = jnp.transpose(cropped.reshape(CROP, col_width, CH), (2, 1, 0))
    for layer_idx in range(NLAYER):
        normed_in = channel_norm(current.astype(jnp.float32)).astype(jnp.bfloat16)
        projected = jnp.einsum(
            "cd,cwi->dwi", proj_weight[layer_idx], normed_in, preferred_element_type=jnp.float32
        )
        left_proj = (jax.nn.sigmoid(projected[:CH]) * projected[CH : 2 * CH] * pair_mask).astype(
            jnp.bfloat16
        )
        right_proj = (
            jax.nn.sigmoid(projected[2 * CH : 3 * CH]) * projected[3 * CH : 4 * CH] * pair_mask
        ).astype(jnp.bfloat16)
        gate_vals = jax.nn.sigmoid(projected[4 * CH :])
        left_send = left_proj.reshape(groups, per_group, col_width, parts_count, part_rows)
        left_send = jnp.transpose(left_send, (0, 3, 1, 2, 4)).reshape(
            row_count, per_group, col_width, part_rows
        )
        right_send = right_proj.reshape(groups, per_group, col_width, parts_count, part_rows)
        right_send = jnp.transpose(right_send, (0, 3, 1, 2, 4)).reshape(
            row_count, per_group, col_width, part_rows
        )
        left_got, right_got = (
            lax.all_to_all(left_send, "row", split_axis=0, concat_axis=2, tiled=True),
            lax.all_to_all(right_send, "row", split_axis=0, concat_axis=2, tiled=True),
        )
        right_whole = right_got[0]
        partner = from_partner(right_whole, "row", 0)
        lower_side = my_index // (1 << 0) % 2 == 0
        right_whole = jnp.where(
            lower_side,
            jnp.concatenate([right_whole, partner], axis=2),
            jnp.concatenate([partner, right_whole], axis=2),
        )
        products = jnp.einsum(
            "cki,ckj->cij", left_got[0], right_whole, preferred_element_type=jnp.float32
        ).astype(jnp.bfloat16)
        back_send = jnp.transpose(
            products.reshape(per_group, part_rows, row_count, col_width), (2, 0, 3, 1)
        )
        back_got = lax.all_to_all(back_send, "row", split_axis=0, concat_axis=0, tiled=True)
        merged = back_got.reshape(groups, parts_count, per_group, col_width, part_rows)
        merged = jnp.transpose(merged, (0, 2, 3, 1, 4)).reshape(CH, col_width, CROP)
        normed_out = channel_norm(merged.astype(jnp.float32)).astype(jnp.bfloat16)
        update = jnp.einsum(
            "cd,cwi->dwi", out_weight[layer_idx], normed_out, preferred_element_type=jnp.float32
        )
        current = (current.astype(jnp.float32) + gate_vals * update).astype(jnp.bfloat16)
    normed_final = channel_norm(current.astype(jnp.float32))
    template_count = lax.axis_size("tmpl")
    summed = lax.psum(normed_final.astype(jnp.bfloat16), "tmpl").astype(jnp.float32)
    hidden = jnp.maximum(summed / template_count, 0.0).astype(jnp.bfloat16)
    result = jnp.einsum(
        "cz,cwi->zwi", final_weight, hidden, preferred_element_type=jnp.float32
    ).astype(jnp.bfloat16)
    return result


def solution(mesh):
    placed = (P("tmpl", "row", None, None), P("tmpl", None), P(), P(), P(), P())
    return jax.shard_map(
        on_device, mesh=mesh, in_specs=placed, out_specs=P(None, "row", None), check_vma=False
    )
```

profile of v0, /device:TPU:1, one launch (start us, length us, event | category | flops | bytes accessed | tf_op | source)
XLA Modules:
  0.0 438.9 jit_solution(15340569308380098732)
XLA Ops:
  7.2 3.6 copy.60
  10.8 3.0 copy.41
  13.9 3.1 gather_fusion
  17.0 3.2 copy.42
  20.2 5.4 %all_to_all.19 = bf16[16,128,512]{2,1,0:T(8,128)(2,1)S(1)} reshape(bf16[16,8,128,64]{3,2,1,0:T(8,128)(2,1)} %copy.42) | data formatting | bytes 4194304 | tf_op jit(solution)/shard_map/all_to_all | solution.py:44
  28.1 17.0 %all-to-all-start = ((bf16[16,128,512]{2,0,1:T(8,128)(2,1)}), bf16[16,128,512]{2,0,1:T(8,128)(2,1)S(1)}, u32[]{:S(2)}, u32[]{:S(2)}) async-start(bf16[16,128,512]{2,0,1:T(8,128)(2,1)} %copy.43), calls=%async_computation | async-start | bytes 4194304 | tf_op jit(solution)/shard_map/all_to_all | solution.py:44
  46.4 4.3 compare_select_fusion.1
  51.5 46.3 %all-to-all-done = bf16[16,128,512]{2,0,1:T(8,128)(2,1)S(1)} async-done(((bf16[16,128,512]{2,0,1:T(8,128)(2,1)}), bf16[16,128,512]{2,0,1:T(8,128)(2,1)S(1)}, u32[]{:S(2)}, u32[]{:S(2)}) %all-to-all-start) | async-done | bytes 2097184 | tf_op jit(solution)/shard_map/all_to_all | solution.py:44
  104.3 2.8 fusion.29
  108.6 2.6 reshape.330
  111.2 3.3 copy.46
  114.5 7.3 %all-to-all-start.2 = ((bf16[128,1,8,512]{3,2,1,0:T(8,128)(2,1)}), bf16[128,1,8,512]{3,2,1,0:T(8,128)(2,1)}, u32[]{:S(2)}, u32[]{:S(2)}) async-start(bf16[128,1,8,512]{3,2,1,0:T(8,128)(2,1)} %bitcast.164), calls=%async_computation.2 | async-start | bytes 2097152 | tf_op jit(solution)/shard_map/all_to_all | solution.py:69
  123.4 3.4 copy.45
  126.8 23.1 %all-to-all-done.2 = bf16[128,1,8,512]{3,2,1,0:T(8,128)(2,1)} async-done(((bf16[128,1,8,512]{3,2,1,0:T(8,128)(2,1)}), bf16[128,1,8,512]{3,2,1,0:T(8,128)(2,1)}, u32[]{:S(2)}, u32[]{:S(2)}) %all-to-all-start.2) | async-done | bytes 1048608 | tf_op jit(solution)/shard_map/all_to_all | solution.py:69
  149.9 6.2 %all-to-all-start.1 = ((bf16[128,1,8,512]{3,2,1,0:T(8,128)(2,1)}), bf16[128,1,8,512]{3,2,1,0:T(8,128)(2,1)S(1)}, u32[]{:S(2)}, u32[]{:S(2)}) async-start(bf16[128,1,8,512]{3,2,1,0:T(8,128)(2,1)} %bitcast.20), calls=%async_computation.1 | async-start | bytes 2097152 | tf_op jit(solution)/shard_map/all_to_all | solution.py:68
  156.8 25.8 %all-to-all-done.1 = bf16[128,1,8,512]{3,2,1,0:T(8,128)(2,1)S(1)} async-done(((bf16[128,1,8,512]{3,2,1,0:T(8,128)(2,1)}), bf16[128,1,8,512]{3,2,1,0:T(8,128)(2,1)S(1)}, u32[]{:S(2)}, u32[]{:S(2)}) %all-to-all-start.1) | async-done | bytes 1048608 | tf_op jit(solution)/shard_map/all_to_all | solution.py:68
  182.6 17.1 %collective-permute-done = bf16[1,1024,512]{2,1,0:T(8,128)(2,1)} collective-permute-done((bf16[1,1024,512]{2,1,0:T(8,128)(2,1)}, bf16[1,1024,512]{2,1,0:T(8,128)(2,1)}, u32[]{:S(2)}, u32[]{:S(2)}) %collective-permute-start) | collective-permute-done | bytes 1048608 | tf_op jit(solution)/shard_map/ppermute | solution.py:17
  199.7 4.5 %fusion.66 = bf16[512,1024]{1,0:T(8,128)(2,1)} fusion(bf16[1024,512]{1,0:T(8,128)(2,1)} %bitcast.26, bf16[1024,512]{1,0:T(8,128)(2,1)} %bitcast.24, pred[]{:T(512)S(6)} %eq.9, bf16[128,1,8,512]{3,2,1,0:T(8,128)(2,1)S(1)} %all-to-all-done.1), kind=kOutput, calls=%fused_computation.95 | convolution fusion | flops 1083703296 | bytes 4194305 | tf_op jit(solution)/shard_map/cki,ckj->cij/dot_general | solution.py:79
  205.7 40.8 %all_to_all.62 = bf16[128,1,8,512]{3,2,1,0:T(8,128)(2,1)S(1)} all-to-all(bf16[128,1,8,512]{3,2,1,0:T(8,128)(2,1)S(1)} %bitcast.167), channel_id=1, replica_groups=mesh['tmpl'=2,'row'=128] {'row'}, dimensions={0} | all-to-all | bytes 2097152 | tf_op jit(solution)/shard_map/all_to_all | solution.py:85
  249.7 2.8 convert_reduce_fusion
  255.9 2.7 copy-done.2
  260.2 3.3 copy.52
  263.5 7.5 %all-to-all-start.5 = ((bf16[128,1,8,512]{3,2,1,0:T(8,128)(2,1)}), bf16[128,1,8,512]{3,2,1,0:T(8,128)(2,1)}, u32[]{:S(2)}, u32[]{:S(2)}) async-start(bf16[128,1,8,512]{3,2,1,0:T(8,128)(2,1)} %bitcast.43), calls=%async_computation.5 | async-start | bytes 2097152 | tf_op jit(solution)/shard_map/all_to_all | solution.py:69
  273.9 23.3 %all-to-all-done.5 = bf16[128,1,8,512]{3,2,1,0:T(8,128)(2,1)} async-done(((bf16[128,1,8,512]{3,2,1,0:T(8,128)(2,1)}), bf16[128,1,8,512]{3,2,1,0:T(8,128)(2,1)}, u32[]{:S(2)}, u32[]{:S(2)}) %all-to-all-start.5) | async-done | bytes 1048608 | tf_op jit(solution)/shard_map/all_to_all | solution.py:69
  297.2 6.2 %all-to-all-start.4 = ((bf16[128,1,8,512]{3,2,1,0:T(8,128)(2,1)}), bf16[128,1,8,512]{3,2,1,0:T(8,128)(2,1)S(1)}, u32[]{:S(2)}, u32[]{:S(2)}) async-start(bf16[128,1,8,512]{3,2,1,0:T(8,128)(2,1)} %bitcast.40), calls=%async_computation.4 | async-start | bytes 2097152 | tf_op jit(solution)/shard_map/all_to_all | solution.py:68
  304.0 24.5 %all-to-all-done.4 = bf16[128,1,8,512]{3,2,1,0:T(8,128)(2,1)S(1)} async-done(((bf16[128,1,8,512]{3,2,1,0:T(8,128)(2,1)}), bf16[128,1,8,512]{3,2,1,0:T(8,128)(2,1)S(1)}, u32[]{:S(2)}, u32[]{:S(2)}) %all-to-all-start.4) | async-done | bytes 1048608 | tf_op jit(solution)/shard_map/all_to_all | solution.py:68
  328.5 17.5 %collective-permute-done.1 = bf16[1,1024,512]{2,1,0:T(8,128)(2,1)S(1)} collective-permute-done((bf16[1,1024,512]{2,1,0:T(8,128)(2,1)}, bf16[1,1024,512]{2,1,0:T(8,128)(2,1)S(1)}, u32[]{:S(2)}, u32[]{:S(2)}) %collective-permute-start.1) | collective-permute-done | bytes 1048608 | tf_op jit(solution)/shard_map/ppermute | solution.py:17
  347.0 3.5 fusion.65
  351.0 39.6 %all_to_all.63 = bf16[128,1,8,512]{3,2,1,0:T(8,128)(2,1)S(1)} all-to-all(bf16[128,1,8,512]{3,2,1,0:T(8,128)(2,1)S(1)} %bitcast.170), channel_id=1, replica_groups=mesh['tmpl'=2,'row'=128] {'row'}, dimensions={0} | all-to-all | bytes 2097152 | tf_op jit(solution)/shard_map/all_to_all | solution.py:85
  393.0 2.6 convert_reduce_fusion.1
  397.2 29.6 %all-reduce.2.cloned.1.call-done = bf16[64,8,1024]{2,0,1:T(8,128)(2,1)} async-done(((bf16[64,8,1024]{2,0,1:T(8,128)(2,1)}), bf16[64,8,1024]{2,0,1:T(8,128)(2,1)}) %all-reduce.2.cloned.1.call-update) | async-done | bytes 1048592 | tf_op jit(solution)/shard_map/psum | solution.py:95
  428.8 2.9 copy.57
  (63 shorter events, 35.4 us)
Async XLA Ops:
  6.5 420.3 %copy-start = (bf16[64,128]{1,0:T(8,128)(2,1)S(1)}, bf16[64,128]{1,0:T(8,128)(2,1)}, u32[]{:S(2)}) copy-start(bf16[64,128]{1,0:T(8,128)(2,1)} %param.11) | copy-start | bytes 49156
  28.1 17.7 %copy-start.4 = (s32[1,8]{1,0:T(1,128)S(1)}, s32[1,8]{1,0:T(1,128)}, u32[]{:S(2)}) copy-start(s32[1,8]{1,0:T(1,128)} %param.7) | copy-start | bytes 100
  28.1 69.7 %all-to-all-start = ((bf16[16,128,512]{2,0,1:T(8,128)(2,1)}), bf16[16,128,512]{2,0,1:T(8,128)(2,1)S(1)}, u32[]{:S(2)}, u32[]{:S(2)}) async-start(bf16[16,128,512]{2,0,1:T(8,128)(2,1)} %copy.43), calls=%async_computation | async-start | bytes 4194304 | tf_op jit(solution)/shard_map/all_to_all | solution.py:44
  101.7 0.9 copy-start.3
  104.3 4.3 copy-start.1
  114.5 35.4 %all-to-all-start.2 = ((bf16[128,1,8,512]{3,2,1,0:T(8,128)(2,1)}), bf16[128,1,8,512]{3,2,1,0:T(8,128)(2,1)}, u32[]{:S(2)}, u32[]{:S(2)}) async-start(bf16[128,1,8,512]{3,2,1,0:T(8,128)(2,1)} %bitcast.164), calls=%async_computation.2 | async-start | bytes 2097152 | tf_op jit(solution)/shard_map/all_to_all | solution.py:69
  149.9 32.7 %all-to-all-start.1 = ((bf16[128,1,8,512]{3,2,1,0:T(8,128)(2,1)}), bf16[128,1,8,512]{3,2,1,0:T(8,128)(2,1)S(1)}, u32[]{:S(2)}, u32[]{:S(2)}) async-start(bf16[128,1,8,512]{3,2,1,0:T(8,128)(2,1)} %bitcast.20), calls=%async_computation.1 | async-start | bytes 2097152 | tf_op jit(solution)/shard_map/all_to_all | solution.py:68
  156.1 43.6 %collective-permute-start = (bf16[1,1024,512]{2,1,0:T(8,128)(2,1)}, bf16[1,1024,512]{2,1,0:T(8,128)(2,1)}, u32[]{:S(2)}, u32[]{:S(2)}) collective-permute-start(bf16[1,1024,512]{2,1,0:T(8,128)(2,1)} %bitcast.25), channel_id=1, source_target_pairs={{0,1},{1,0},{2,3},{3,2},{4,5},{5,4},{6,7},{7,6},{8,9},{9,8},{10,11... | collective-permute-start | bytes 3145736 | tf_op jit(solution)/shard_map/ppermute | solution.py:17
  247.3 2.4 copy-start.6
  254.6 4.0 copy-start.2
  263.5 33.7 %all-to-all-start.5 = ((bf16[128,1,8,512]{3,2,1,0:T(8,128)(2,1)}), bf16[128,1,8,512]{3,2,1,0:T(8,128)(2,1)}, u32[]{:S(2)}, u32[]{:S(2)}) async-start(bf16[128,1,8,512]{3,2,1,0:T(8,128)(2,1)} %bitcast.43), calls=%async_computation.5 | async-start | bytes 2097152 | tf_op jit(solution)/shard_map/all_to_all | solution.py:69
  297.2 31.3 %all-to-all-start.4 = ((bf16[128,1,8,512]{3,2,1,0:T(8,128)(2,1)}), bf16[128,1,8,512]{3,2,1,0:T(8,128)(2,1)S(1)}, u32[]{:S(2)}, u32[]{:S(2)}) async-start(bf16[128,1,8,512]{3,2,1,0:T(8,128)(2,1)} %bitcast.40), calls=%async_computation.4 | async-start | bytes 2097152 | tf_op jit(solution)/shard_map/all_to_all | solution.py:68
  303.4 123.5 %all-reduce.2.cloned.1.call-start = ((), (), s32[]{:S(2)}) async-start(), calls=%async_computation.7 | async-start | bytes 2097152 | tf_op jit(solution)/shard_map/psum | solution.py:95
  303.4 42.6 %collective-permute-start.1 = (bf16[1,1024,512]{2,1,0:T(8,128)(2,1)}, bf16[1,1024,512]{2,1,0:T(8,128)(2,1)S(1)}, u32[]{:S(2)}, u32[]{:S(2)}) collective-permute-start(bf16[1,1024,512]{2,1,0:T(8,128)(2,1)} %bitcast.45), channel_id=1, source_target_pairs={{0,1},{1,0},{2,3},{3,2},{4,5},{5,4},{6,7},{7,6},{8,9},{9,8},{10,11... | collective-permute-start | bytes 3145736 | tf_op jit(solution)/shard_map/ppermute | solution.py:17
  346.0 1.0 copy-start.5
Sparse Core Ops, SparseCore 0:
  397.3 29.4 all-reduce.1
where the time goes:
time: 445 us; the launch traced here: 439 us
  waiting for transfers between devices  207 us (47%)
  blocking collectives  80.3 us (18%)
  local copies, waits for them, and re-layouts  58.5 us (13%)
  starting transfers between devices  45.5 us (10%)
  matrix products  18.7 us (4%)
  between operations  14.7 us (3%)
  other arithmetic  13.9 us (3%)
    all_to_all x2, blocking collectives, on_device(): lax.all_to_all(back_send, 'row', split_axis=0, concat_axis=0, tiled=True)  80.3 us
    all_to_all x2, waiting for transfers between devices, on_device(): lax.all_to_all(left_send, 'row', split_axis=0, concat_axis=2, tiled=True)  50.3 us
    all_to_all x2, waiting for transfers between devices, on_device(): lax.all_to_all(right_send, 'row', split_axis=0, concat_axis=2, tiled=True)  46.3 us
    all_to_all x1, waiting for transfers between devices, on_device(): lax.all_to_all(columns, 'row', split_axis=1, concat_axis=0, tiled=True)  46.3 us
    ppermute x2, waiting for transfers between devices, from_partner(): return lax.ppermute(value, axis, pairs)  34.6 us
    psum x1, waiting for transfers between devices, on_device(): lax.psum(normed_final.astype(jnp.bfloat16), 'tmpl').astype(jnp.float32)  29.6 us
    all_to_all x1, starting transfers between devices, on_device(): lax.all_to_all(columns, 'row', split_axis=1, concat_axis=0, tiled=True)  17 us
    all_to_all x2, starting transfers between devices, on_device(): lax.all_to_all(right_send, 'row', split_axis=0, concat_axis=2, tiled=True)  14.8 us
  transfers between devices with their start and end apart: 8, of which 8 were waited for; matrix products, arithmetic and copies ran while one was open for 3% of the time, Pallas kernels for 0%

commit v1 on v0

--- a/solution.py
+++ b/solution.py
@@ -9,6 +9,12 @@
 NLAYER = 2
 FULL = 2048
 EPSILON = 1e-05
+
+
+def summed_here(value, axis):
+    parts = lax.all_gather(value, axis, axis=0, tiled=False)
+    total = parts.sum(axis=0)
+    return total
 
 
 def from_partner(value, axis, bit):
@@ -92,7 +98,7 @@
         current = (current.astype(jnp.float32) + gate_vals * update).astype(jnp.bfloat16)
     normed_final = channel_norm(current.astype(jnp.float32))
     template_count = lax.axis_size("tmpl")
-    summed = lax.psum(normed_final.astype(jnp.bfloat16), "tmpl").astype(jnp.float32)
+    summed = summed_here(normed_final.astype(jnp.bfloat16), "tmpl").astype(jnp.float32)
     hidden = jnp.maximum(summed / template_count, 0.0).astype(jnp.bfloat16)
     result = jnp.einsum(
         "cz,cwi->zwi", final_weight, hidden, preferred_element_type=jnp.float32

time: 445 us -> 432 us (0.971)
  waiting for transfers between devices: 207 us -> 193 us
    psum x1 -> x0, waiting for transfers between devices: 29.6 us -> none  [on_device(): lax.psum(normed_final.astype(jnp.bfloat16), 'tmpl').astype(jnp.float32)]
    all_gather x0 -> x1, waiting for transfers between devices: none -> 15.1 us  [summed_here(): parts = lax.all_gather(value, axis, axis=0, tiled=False)]
where the time goes in v1:
time: 432 us; the launch traced here: 425 us
  waiting for transfers between devices  193 us (45%)
  blocking collectives  80.3 us (19%)
  local copies, waits for them, and re-layouts  58.5 us (14%)
  starting transfers between devices  45.5 us (11%)
  matrix products  17.5 us (4%)
  other arithmetic  16.1 us (4%)
  between operations  14.7 us (3%)
    all_to_all x2, blocking collectives, on_device(): lax.all_to_all(back_send, 'row', split_axis=0, concat_axis=0, tiled=True)  80.3 us
    all_to_all x2, waiting for transfers between devices, on_device(): lax.all_to_all(left_send, 'row', split_axis=0, concat_axis=2, tiled=True)  50.3 us
    all_to_all x2, waiting for transfers between devices, on_device(): lax.all_to_all(right_send, 'row', split_axis=0, concat_axis=2, tiled=True)  46.3 us
    all_to_all x1, waiting for transfers between devices, on_device(): lax.all_to_all(columns, 'row', split_axis=1, concat_axis=0, tiled=True)  46.3 us
    ppermute x2, waiting for transfers between devices, from_partner(): return lax.ppermute(value, axis, pairs)  34.6 us
    all_to_all x1, starting transfers between devices, on_device(): lax.all_to_all(columns, 'row', split_axis=1, concat_axis=0, tiled=True)  17 us
    all_gather x1, waiting for transfers between devices, summed_here(): parts = lax.all_gather(value, axis, axis=0, tiled=False)  15.1 us
    all_to_all x2, starting transfers between devices, on_device(): lax.all_to_all(right_send, 'row', split_axis=0, concat_axis=2, tiled=True)  14.8 us
  transfers between devices with their start and end apart: 8, of which 8 were waited for; matrix products, arithmetic and copies ran while one was open for 3% of the time, Pallas kernels for 0%

profile of v1, /device:TPU:1, one launch (start us, length us, event | category | flops | bytes accessed | tf_op | source)
XLA Modules:
  0.0 425.4 jit_solution(4491461182885584837)
XLA Ops:
  7.2 3.6 copy.60
  10.8 3.0 copy.41
  13.9 3.1 gather_fusion
  17.0 3.2 copy.42
  20.2 5.4 %all_to_all.19 = bf16[16,128,512]{2,1,0:T(8,128)(2,1)S(1)} reshape(bf16[16,8,128,64]{3,2,1,0:T(8,128)(2,1)} %copy.42) | data formatting | bytes 4194304 | tf_op jit(solution)/shard_map/all_to_all | solution.py:50
  28.1 17.0 %all-to-all-start = ((bf16[16,128,512]{2,0,1:T(8,128)(2,1)}), bf16[16,128,512]{2,0,1:T(8,128)(2,1)S(1)}, u32[]{:S(2)}, u32[]{:S(2)}) async-start(bf16[16,128,512]{2,0,1:T(8,128)(2,1)} %copy.43), calls=%async_computation | async-start | bytes 4194304 | tf_op jit(solution)/shard_map/all_to_all | solution.py:50
  46.4 4.3 %compare_select_fusion.1 = s32[1024,1]{0,1:T(1,128)S(1)} fusion(s32[]{:T(128)} %bitcast.10, s32[]{:T(128)} %bitcast.11, s32[]{:T(128)} %bitcast.12, s32[]{:T(128)} %bitcast.13, s32[]{:T(128)} %bitcast.14, s32[]{:T(128)} %bitcast.16, s32[]{:T(128)} %bitcast.15), kind=kLoop, calls=%fused_computation.126 | loop fusion | flops 23552 | bytes 4124 | tf_op jit(solution)/shard_map/gather | solution.py:44
  51.5 46.3 %all-to-all-done = bf16[16,128,512]{2,0,1:T(8,128)(2,1)S(1)} async-done(((bf16[16,128,512]{2,0,1:T(8,128)(2,1)}), bf16[16,128,512]{2,0,1:T(8,128)(2,1)S(1)}, u32[]{:S(2)}, u32[]{:S(2)}) %all-to-all-start) | async-done | bytes 2097184 | tf_op jit(solution)/shard_map/all_to_all | solution.py:50
  104.3 2.8 fusion.29
  108.6 2.6 reshape.330
  111.2 3.3 copy.46
  114.5 7.3 %all-to-all-start.2 = ((bf16[128,1,8,512]{3,2,1,0:T(8,128)(2,1)}), bf16[128,1,8,512]{3,2,1,0:T(8,128)(2,1)}, u32[]{:S(2)}, u32[]{:S(2)}) async-start(bf16[128,1,8,512]{3,2,1,0:T(8,128)(2,1)} %bitcast.165), calls=%async_computation.2 | async-start | bytes 2097152 | tf_op jit(solution)/shard_map/all_to_all | solution.py:75
  123.4 3.4 copy.45
  126.8 23.1 %all-to-all-done.2 = bf16[128,1,8,512]{3,2,1,0:T(8,128)(2,1)} async-done(((bf16[128,1,8,512]{3,2,1,0:T(8,128)(2,1)}), bf16[128,1,8,512]{3,2,1,0:T(8,128)(2,1)}, u32[]{:S(2)}, u32[]{:S(2)}) %all-to-all-start.2) | async-done | bytes 1048608 | tf_op jit(solution)/shard_map/all_to_all | solution.py:75
  149.9 6.2 %all-to-all-start.1 = ((bf16[128,1,8,512]{3,2,1,0:T(8,128)(2,1)}), bf16[128,1,8,512]{3,2,1,0:T(8,128)(2,1)S(1)}, u32[]{:S(2)}, u32[]{:S(2)}) async-start(bf16[128,1,8,512]{3,2,1,0:T(8,128)(2,1)} %bitcast.20), calls=%async_computation.1 | async-start | bytes 2097152 | tf_op jit(solution)/shard_map/all_to_all | solution.py:74
  156.8 25.8 %all-to-all-done.1 = bf16[128,1,8,512]{3,2,1,0:T(8,128)(2,1)S(1)} async-done(((bf16[128,1,8,512]{3,2,1,0:T(8,128)(2,1)}), bf16[128,1,8,512]{3,2,1,0:T(8,128)(2,1)S(1)}, u32[]{:S(2)}, u32[]{:S(2)}) %all-to-all-start.1) | async-done | bytes 1048608 | tf_op jit(solution)/shard_map/all_to_all | solution.py:74
  182.6 17.1 %collective-permute-done = bf16[1,1024,512]{2,1,0:T(8,128)(2,1)} collective-permute-done((bf16[1,1024,512]{2,1,0:T(8,128)(2,1)}, bf16[1,1024,512]{2,1,0:T(8,128)(2,1)}, u32[]{:S(2)}, u32[]{:S(2)}) %collective-permute-start) | collective-permute-done | bytes 1048608 | tf_op jit(solution)/shard_map/ppermute | solution.py:23
  199.7 4.5 %fusion.66 = bf16[512,1024]{1,0:T(8,128)(2,1)} fusion(bf16[1024,512]{1,0:T(8,128)(2,1)} %bitcast.26, bf16[1024,512]{1,0:T(8,128)(2,1)} %bitcast.24, pred[]{:T(512)S(6)} %eq.9, bf16[128,1,8,512]{3,2,1,0:T(8,128)(2,1)S(1)} %all-to-all-done.1), kind=kOutput, calls=%fused_computation.95 | convolution fusion | flops 1083703296 | bytes 4194305 | tf_op jit(solution)/shard_map/cki,ckj->cij/dot_general | solution.py:85
  205.7 40.8 %all_to_all.62 = bf16[128,1,8,512]{3,2,1,0:T(8,128)(2,1)S(1)} all-to-all(bf16[128,1,8,512]{3,2,1,0:T(8,128)(2,1)S(1)} %bitcast.168), channel_id=1, replica_groups=mesh['tmpl'=2,'row'=128] {'row'}, dimensions={0} | all-to-all | bytes 2097152 | tf_op jit(solution)/shard_map/all_to_all | solution.py:91
  249.7 2.8 convert_reduce_fusion
  255.9 2.7 copy-done.2
  260.2 3.3 copy.52
  263.5 7.5 %all-to-all-start.5 = ((bf16[128,1,8,512]{3,2,1,0:T(8,128)(2,1)}), bf16[128,1,8,512]{3,2,1,0:T(8,128)(2,1)}, u32[]{:S(2)}, u32[]{:S(2)}) async-start(bf16[128,1,8,512]{3,2,1,0:T(8,128)(2,1)} %bitcast.43), calls=%async_computation.5 | async-start | bytes 2097152 | tf_op jit(solution)/shard_map/all_to_all | solution.py:75
  273.9 23.3 %all-to-all-done.5 = bf16[128,1,8,512]{3,2,1,0:T(8,128)(2,1)} async-done(((bf16[128,1,8,512]{3,2,1,0:T(8,128)(2,1)}), bf16[128,1,8,512]{3,2,1,0:T(8,128)(2,1)}, u32[]{:S(2)}, u32[]{:S(2)}) %all-to-all-start.5) | async-done | bytes 1048608 | tf_op jit(solution)/shard_map/all_to_all | solution.py:75
  297.2 6.2 %all-to-all-start.4 = ((bf16[128,1,8,512]{3,2,1,0:T(8,128)(2,1)}), bf16[128,1,8,512]{3,2,1,0:T(8,128)(2,1)S(1)}, u32[]{:S(2)}, u32[]{:S(2)}) async-start(bf16[128,1,8,512]{3,2,1,0:T(8,128)(2,1)} %bitcast.40), calls=%async_computation.4 | async-start | bytes 2097152 | tf_op jit(solution)/shard_map/all_to_all | solution.py:74
  304.0 24.5 %all-to-all-done.4 = bf16[128,1,8,512]{3,2,1,0:T(8,128)(2,1)S(1)} async-done(((bf16[128,1,8,512]{3,2,1,0:T(8,128)(2,1)}), bf16[128,1,8,512]{3,2,1,0:T(8,128)(2,1)S(1)}, u32[]{:S(2)}, u32[]{:S(2)}) %all-to-all-start.4) | async-done | bytes 1048608 | tf_op jit(solution)/shard_map/all_to_all | solution.py:74
  328.5 17.5 %collective-permute-done.1 = bf16[1,1024,512]{2,1,0:T(8,128)(2,1)S(1)} collective-permute-done((bf16[1,1024,512]{2,1,0:T(8,128)(2,1)}, bf16[1,1024,512]{2,1,0:T(8,128)(2,1)S(1)}, u32[]{:S(2)}, u32[]{:S(2)}) %collective-permute-start.1) | collective-permute-done | bytes 1048608 | tf_op jit(solution)/shard_map/ppermute | solution.py:23
  347.0 3.5 fusion.65
  351.0 39.6 %all_to_all.63 = bf16[128,1,8,512]{3,2,1,0:T(8,128)(2,1)S(1)} all-to-all(bf16[128,1,8,512]{3,2,1,0:T(8,128)(2,1)S(1)} %bitcast.171), channel_id=1, replica_groups=mesh['tmpl'=2,'row'=128] {'row'}, dimensions={0} | all-to-all | bytes 2097152 | tf_op jit(solution)/shard_map/all_to_all | solution.py:91
  393.0 2.6 convert_reduce_fusion.1
  397.2 15.1 %all-gather.3.cloned.1.call-done = bf16[128,8,1024]{2,0,1:T(8,128)(2,1)} async-done(((bf16[64,8,1024]{2,0,1:T(8,128)(2,1)}), bf16[128,8,1024]{2,0,1:T(8,128)(2,1)}) %all-gather.3.cloned.1.call-update) | async-done | bytes 2097168 | tf_op jit(solution)/shard_map/all_gather | solution.py:15
  415.4 2.9 copy.57
  (64 shorter events, 36.4 us)
Async XLA Ops:
  6.5 408.0 %copy-start = (bf16[64,128]{1,0:T(8,128)(2,1)S(1)}, bf16[64,128]{1,0:T(8,128)(2,1)}, u32[]{:S(2)}) copy-start(bf16[64,128]{1,0:T(8,128)(2,1)} %param.11) | copy-start | bytes 49156
  28.1 17.7 %copy-start.4 = (s32[1,8]{1,0:T(1,128)S(1)}, s32[1,8]{1,0:T(1,128)}, u32[]{:S(2)}) copy-start(s32[1,8]{1,0:T(1,128)} %param.7) | copy-start | bytes 100
  28.1 69.7 %all-to-all-start = ((bf16[16,128,512]{2,0,1:T(8,128)(2,1)}), bf16[16,128,512]{2,0,1:T(8,128)(2,1)S(1)}, u32[]{:S(2)}, u32[]{:S(2)}) async-start(bf16[16,128,512]{2,0,1:T(8,128)(2,1)} %copy.43), calls=%async_computation | async-start | bytes 4194304 | tf_op jit(solution)/shard_map/all_to_all | solution.py:50
  101.7 0.9 copy-start.3
  104.3 4.3 %copy-start.1 = (f32[320,8,1024]{2,0,1:T(8,128)}, f32[320,8,1024]{2,0,1:T(8,128)S(1)}, u32[]{:S(2)}) copy-start(f32[320,8,1024]{2,0,1:T(8,128)S(1)} %convolution_bitcast_fusion.1) | copy-start | bytes 31457284
  114.5 35.4 %all-to-all-start.2 = ((bf16[128,1,8,512]{3,2,1,0:T(8,128)(2,1)}), bf16[128,1,8,512]{3,2,1,0:T(8,128)(2,1)}, u32[]{:S(2)}, u32[]{:S(2)}) async-start(bf16[128,1,8,512]{3,2,1,0:T(8,128)(2,1)} %bitcast.165), calls=%async_computation.2 | async-start | bytes 2097152 | tf_op jit(solution)/shard_map/all_to_all | solution.py:75
  149.9 32.7 %all-to-all-start.1 = ((bf16[128,1,8,512]{3,2,1,0:T(8,128)(2,1)}), bf16[128,1,8,512]{3,2,1,0:T(8,128)(2,1)S(1)}, u32[]{:S(2)}, u32[]{:S(2)}) async-start(bf16[128,1,8,512]{3,2,1,0:T(8,128)(2,1)} %bitcast.20), calls=%async_computation.1 | async-start | bytes 2097152 | tf_op jit(solution)/shard_map/all_to_all | solution.py:74
  156.1 43.6 %collective-permute-start = (bf16[1,1024,512]{2,1,0:T(8,128)(2,1)}, bf16[1,1024,512]{2,1,0:T(8,128)(2,1)}, u32[]{:S(2)}, u32[]{:S(2)}) collective-permute-start(bf16[1,1024,512]{2,1,0:T(8,128)(2,1)} %bitcast.25), channel_id=1, source_target_pairs={{0,1},{1,0},{2,3},{3,2},{4,5},{5,4},{6,7},{7,6},{8,9},{9,8},{10,11... | collective-permute-start | bytes 3145736 | tf_op jit(solution)/shard_map/ppermute | solution.py:23
  247.3 2.4 copy-start.6
  254.6 4.0 copy-start.2
  263.5 33.7 %all-to-all-start.5 = ((bf16[128,1,8,512]{3,2,1,0:T(8,128)(2,1)}), bf16[128,1,8,512]{3,2,1,0:T(8,128)(2,1)}, u32[]{:S(2)}, u32[]{:S(2)}) async-start(bf16[128,1,8,512]{3,2,1,0:T(8,128)(2,1)} %bitcast.43), calls=%async_computation.5 | async-start | bytes 2097152 | tf_op jit(solution)/shard_map/all_to_all | solution.py:75
  297.2 31.3 %all-to-all-start.4 = ((bf16[128,1,8,512]{3,2,1,0:T(8,128)(2,1)}), bf16[128,1,8,512]{3,2,1,0:T(8,128)(2,1)S(1)}, u32[]{:S(2)}, u32[]{:S(2)}) async-start(bf16[128,1,8,512]{3,2,1,0:T(8,128)(2,1)} %bitcast.40), calls=%async_computation.4 | async-start | bytes 2097152 | tf_op jit(solution)/shard_map/all_to_all | solution.py:74
  303.4 109.0 %all-gather.3.cloned.1.call-start = ((), (), s32[]{:S(2)}) async-start(), calls=%async_computation.7 | async-start | bytes 3145728 | tf_op jit(solution)/shard_map/all_gather | solution.py:15
  303.4 42.6 %collective-permute-start.1 = (bf16[1,1024,512]{2,1,0:T(8,128)(2,1)}, bf16[1,1024,512]{2,1,0:T(8,128)(2,1)S(1)}, u32[]{:S(2)}, u32[]{:S(2)}) collective-permute-start(bf16[1,1024,512]{2,1,0:T(8,128)(2,1)} %bitcast.45), channel_id=1, source_target_pairs={{0,1},{1,0},{2,3},{3,2},{4,5},{5,4},{6,7},{7,6},{8,9},{9,8},{10,11... | collective-permute-start | bytes 3145736 | tf_op jit(solution)/shard_map/ppermute | solution.py:23
  346.0 1.0 copy-start.5
Sparse Core Ops, SparseCore 0:
  397.3 14.9 all-gather.2
